TPU v7x, 512 devices: a whole 4x4x16 slice. The times are simulated.
512 devices in a mesh: band: 128 (over z_lo, y, x, core), head: 4 (over z_hi).
Axes of the slice: x: 4, y: 4, z: 16 (z_hi: 4, z_lo: 4; z = z_hi * 4 + z_lo), core: 2. Of those that a mesh axis runs over, the one named last changes fastest.
Arguments:
- queries: bfloat16 [256, 131072], P('head', 'band'), may hold values from -76 to 76
- keys: bfloat16 [256, 131072], P('head', 'band'), may hold values from -6 to 6
- values: bfloat16 [256, 131072], P('head', 'band'), may hold values from -6 to 6
- grad_out: bfloat16 [256, 131072], P('head', 'band'), may hold values from -6 to 6
- w_out: bfloat16 [256, 256], P('head'), may hold values from -0.375 to 0.375
- key_lists: int32 [1024, 8], P('band'), may hold values from 0 to 1023, as said below
- key_counts: int32 [1024], P('band'), may hold values from 2 to 8, as said below
Outputs:
- grad_queries: bfloat16 [256, 131072], P('head', 'band')
- grad_keys: bfloat16 [256, 131072], P('head', 'band')
- grad_values: bfloat16 [256, 131072], P('head', 'band')
- grad_w_out: float32 [256, 256], P('head')
Inputs may be any that keep to these rules, and one draw needn't show every extreme that they name: `key_lists`: row b holds 8 different blocks; the first is b itself and every entry lies within 8 blocks of b. `key_counts`: the number of leading entries of the row of key_lists that are used.
All inputs are finite; a program needn't handle non-finite values.
Results may differ from a plain program's by a relative error of at most 0.0058.
Values may be sent and summed in bfloat16 or wider, within the bound.
A program may use at most 64 MiB of HBM per device.

v0:
```python
import jax
import jax.numpy as jnp
from jax import lax
from jax.sharding import PartitionSpec as P

HEAD_DIM = 32
BLOCK = 128
REACH = 4
MAX_KEYS = 8


def with_halo(block, sides, width):
    for axis, dim in sides:
        count = lax.axis_size(axis)
        forward = [(i, i + 1) for i in range(count - 1)]
        backward = [(target, source) for source, target in forward]
        low = lax.ppermute(
            lax.slice_in_dim(block, block.shape[dim] - width, None, axis=dim), axis, forward
        )
        high = lax.ppermute(lax.slice_in_dim(block, 0, width, axis=dim), axis, backward)
        block = jnp.concatenate([low, block, high], axis=dim)
    return block


def shifted(value, axis, steps):
    count = lax.axis_size(axis)
    initial, last = (max(0, -steps), min(count, count - steps))
    return lax.ppermute(value, axis, [(source, source + steps) for source in range(initial, last)])


def block_grads(query_blk, grad_blk, slots, usable, key_ext, value_ext, bias_ext):
    count = slots.shape[0]
    span = count * BLOCK
    chans = query_blk.shape[0]
    heads_here = chans // HEAD_DIM
    scale = HEAD_DIM ** (-0.5)
    picked_k = key_ext[:, slots].reshape(heads_here, HEAD_DIM, span)
    picked_v = value_ext[:, slots].reshape(heads_here, HEAD_DIM, span)
    key_bias = bias_ext[slots].reshape(span)
    live_keys = jnp.repeat(usable, BLOCK)
    query_h = query_blk.reshape(heads_here, HEAD_DIM, BLOCK)
    grad_h = grad_blk.reshape(heads_here, HEAD_DIM, BLOCK)
    scores = (
        jnp.einsum("hdq,hdk->hqk", query_h, picked_k, preferred_element_type=jnp.float32) * scale
        + key_bias
    )
    scores = jnp.where(live_keys, scores, -jnp.inf)
    peak = jnp.max(scores, axis=-1)
    log_total = peak + jnp.log(jnp.sum(jnp.exp(scores - peak[..., None]), axis=-1))
    probs = jnp.exp(scores - log_total[..., None])
    probs_low = probs.astype(jnp.bfloat16)
    dprobs = jnp.einsum("hdq,hdk->hqk", grad_h, picked_v, preferred_element_type=jnp.float32)
    spread = jnp.sum(probs * dprobs, axis=-1)
    dscores = (probs * (dprobs - spread[..., None]) * scale).astype(jnp.bfloat16)
    dquery = jnp.einsum(
        "hqk,hdk->hdq", dscores, picked_k, preferred_element_type=jnp.float32
    ).reshape(chans, BLOCK)
    dkey = jnp.einsum("hqk,hdq->hdk", dscores, query_h, preferred_element_type=jnp.float32).reshape(
        chans, count, BLOCK
    )
    dvalue = jnp.einsum(
        "hqk,hdq->hdk", probs_low, grad_h, preferred_element_type=jnp.float32
    ).reshape(chans, count, BLOCK)
    attended = jnp.einsum(
        "hqk,hdk->hdq", probs_low, picked_v, preferred_element_type=jnp.float32
    ).reshape(chans, BLOCK)
    return (dquery, dkey, dvalue, attended, log_total, spread)


def band_bias(first_block, ext_blocks, total_tokens):
    positions = first_block * BLOCK + jnp.arange(ext_blocks * BLOCK, dtype=jnp.int32)
    positions = jnp.clip(positions, 0, total_tokens - 1).astype(jnp.float32)
    return jnp.log(jnp.sin(jnp.pi * (positions + 0.5) / total_tokens)).reshape(ext_blocks, BLOCK)


def run_blocks(query_blocks, grad_blocks, slot_rows, use_rows, key_ext, value_ext, bias_ext):
    chans = query_blocks.shape[0]
    nblocks = query_blocks.shape[1]
    heads_here = chans // HEAD_DIM
    ext_blocks = key_ext.shape[1]
    zeros = jnp.zeros((chans, ext_blocks, BLOCK), jnp.float32)
    start = (
        zeros,
        zeros,
        jnp.zeros((chans, nblocks, BLOCK), jnp.bfloat16),
        jnp.zeros((chans, nblocks, BLOCK), jnp.bfloat16),
        jnp.zeros((nblocks, heads_here, BLOCK), jnp.float32),
        jnp.zeros((nblocks, heads_here, BLOCK), jnp.float32),
    )

    def run_width(index, carry):
        acc_k, acc_v, dq_all, att_all, lse_all, spread_all = carry
        query_blk = lax.dynamic_index_in_dim(query_blocks, index, 1, keepdims=False)
        grad_blk = lax.dynamic_index_in_dim(grad_blocks, index, 1, keepdims=False)
        slots = slot_rows[index]
        dquery, dkey, dvalue, attended, log_total, spread = block_grads(
            query_blk, grad_blk, slots, use_rows[index], key_ext, value_ext, bias_ext
        )
        acc_k = acc_k.at[:, slots].add(dkey)
        acc_v = acc_v.at[:, slots].add(dvalue)
        dq_all = dq_all.at[:, index].set(dquery.astype(jnp.bfloat16))
        att_all = att_all.at[:, index].set(attended.astype(jnp.bfloat16))
        lse_all = lse_all.at[index].set(log_total)
        spread_all = spread_all.at[index].set(spread)
        return (acc_k, acc_v, dq_all, att_all, lse_all, spread_all)

    def block_step(index, carry):
        return run_width(index, carry)

    return lax.fori_loop(0, nblocks, block_step, start)


def shards(queries, keys, values, grad_out, w_out, key_lists, key_counts):
    chans = queries.shape[0]
    blocks = queries.shape[1] // BLOCK
    rim_blocks = 2 * REACH
    ext_blocks = blocks + 2 * rim_blocks
    band_index = lax.axis_index("band")
    band_count = lax.axis_size("band")
    total_tokens = blocks * BLOCK * band_count
    full_grad = lax.all_gather(grad_out, "head", axis=0, tiled=True)
    grad_att = jnp.einsum("cd,dt->ct", w_out, full_grad, preferred_element_type=jnp.float32).astype(
        jnp.bfloat16
    )
    key_pairs = jnp.stack(
        [keys.reshape(chans, blocks, BLOCK), values.reshape(chans, blocks, BLOCK)]
    )
    pair_ext = with_halo(key_pairs, (("band", 2),), rim_blocks)
    key_ext = pair_ext[0]
    value_ext = pair_ext[1]
    first_block = band_index * blocks - rim_blocks
    bias_ext = band_bias(first_block, ext_blocks, total_tokens)
    slot_ids = jnp.arange(MAX_KEYS, dtype=jnp.int32)
    masked = jnp.where(slot_ids[None, :] < key_counts[:, None], key_lists, -1)
    usable = masked >= 0
    local_slots = jnp.clip(masked - first_block, 0, ext_blocks - 1)
    query_blocks = queries.reshape(chans, blocks, BLOCK)
    grad_blocks = grad_att.reshape(chans, blocks, BLOCK)
    acc_k, acc_v, dq_all, att_all, lse_all, spread_all = run_blocks(
        query_blocks, grad_blocks, local_slots, usable, key_ext, value_ext, bias_ext
    )
    lower_part = jnp.stack([acc_k[:, :rim_blocks], acc_v[:, :rim_blocks]])
    upper_part = jnp.stack([acc_k[:, rim_blocks + blocks :], acc_v[:, rim_blocks + blocks :]])
    from_above = shifted(lower_part.astype(jnp.bfloat16), "band", -1).astype(lower_part.dtype)
    from_below = shifted(upper_part.astype(jnp.bfloat16), "band", 1).astype(upper_part.dtype)
    owned = jnp.stack(
        [acc_k[:, rim_blocks : rim_blocks + blocks], acc_v[:, rim_blocks : rim_blocks + blocks]]
    )
    owned = owned.at[:, :, :rim_blocks].add(from_below)
    owned = owned.at[:, :, blocks - rim_blocks :].add(from_above)
    grad_queries = dq_all.reshape(chans, blocks * BLOCK)
    grad_keys = owned[0].reshape(chans, blocks * BLOCK).astype(jnp.bfloat16)
    grad_values = owned[1].reshape(chans, blocks * BLOCK).astype(jnp.bfloat16)
    attended = att_all.reshape(chans, blocks * BLOCK)
    partial_w = jnp.einsum("ct,dt->cd", attended, full_grad, preferred_element_type=jnp.float32)
    grad_w_out = lax.psum(partial_w, "band")
    return (grad_queries, grad_keys, grad_values, grad_w_out)


def solution(mesh):
    in_specs = (
        P("head", "band"),
        P("head", "band"),
        P("head", "band"),
        P("head", "band"),
        P("head", None),
        P("band", None),
        P("band"),
    )
    out_specs = (P("head", "band"), P("head", "band"), P("head", "band"), P("head", None))
    return jax.shard_map(shards, mesh=mesh, in_specs=in_specs, out_specs=out_specs, check_vma=False)
```

profile of v0, /device:TPU:128, one launch (start us, length us, event | category | flops | bytes accessed | tf_op | source)
XLA Modules:
  0.0 1363.9 jit_solution(3524123765928324000)
XLA Ops:
  10.5 3.0 collective-permute-start
  14.9 28.8 %all_gather.3 = bf16[256,1024]{1,0:T(8,128)(2,1)S(1)} all-gather(bf16[64,1024]{1,0:T(8,128)(2,1)S(1)} %copy-done.10), channel_id=1, replica_groups=mesh['band'=128,'head'=4] {'head'}, dimensions={0}, use_global_device_ids=true | all-gather | bytes 655360 | tf_op jit(solution)/shard_map/all_gather | solution.py:121
  48.4 139.9 %while.26 = (s32[]{:T(128)}, f32[64,24,128]{2,0,1:T(8,128)}, f32[64,24,128]{2,0,1:T(8,128)S(1)}, bf16[64,8,128]{2,0,1:T(8,128)(2,1)S(1)}, bf16[64,8,128]{2,0,1:T...) while((s32[]{:T(128)}, f32[64,24,128]{2,0,1:T(8,128)}, ...), condition=%wide.region_7.8_spmd.clone, body=%wide.region_0.7_spmd.clone.sunk | while | flops 107143464 | bytes 23508944 | solution.py:110
  52.6 1.6 gather_fusion.2
  54.3 1.6 gather_fusion
  60.1 1.8 fusion.90
  62.0 2.0 constant_dynamic-update-slice_fusion.3
  70.1 1.6 gather_fusion.2
  71.8 1.6 gather_fusion
  77.5 1.8 fusion.90
  79.5 2.0 constant_dynamic-update-slice_fusion.3
  87.6 1.6 gather_fusion.2
  95.0 1.8 fusion.90
  97.0 2.0 constant_dynamic-update-slice_fusion.3
  105.0 1.6 gather_fusion.2
  112.5 1.8 fusion.90
  114.5 2.0 constant_dynamic-update-slice_fusion.3
  122.5 1.6 gather_fusion.2
  130.0 1.8 fusion.90
  131.9 2.0 constant_dynamic-update-slice_fusion.3
  140.0 1.6 gather_fusion.2
  147.5 1.8 fusion.90
  149.4 2.0 constant_dynamic-update-slice_fusion.3
  157.5 1.6 gather_fusion.2
  164.9 1.8 fusion.90
  166.9 2.0 constant_dynamic-update-slice_fusion.3
  175.0 1.6 gather_fusion.2
  182.4 1.8 fusion.90
  184.4 2.0 constant_dynamic-update-slice_fusion.3
  188.2 2.1 fusion.34
  191.9 3.0 collective-permute-start.2
  197.8 1157.8 %all-reduce.2.cloned.1.call-done = f32[64,256]{1,0:T(8,128)} async-done(((f32[64,256]{1,0:T(8,128)}), f32[64,256]{1,0:T(8,128)}) %all-reduce.2.cloned.1.call-update) | async-done | bytes 65552 | tf_op jit(solution)/shard_map/psum | solution.py:156
  (411 shorter events, 106.6 us)
Async XLA Ops:
  7.2 36.8 %copy-start = (bf16[64,1024]{1,0:T(8,128)(2,1)S(1)}, bf16[64,1024]{1,0:T(8,128)(2,1)}, u32[]{:S(2)}) copy-start(bf16[64,1024]{1,0:T(8,128)(2,1)} %param.21) | copy-start | bytes 393220
  7.2 6.4 copy-start.15
  7.2 6.4 copy-start.14
  7.2 7.7 copy-start.10
  7.2 36.5 %copy-start.13 = (bf16[64,256]{1,0:T(8,128)(2,1)S(1)}, bf16[64,256]{1,0:T(8,128)(2,1)}, u32[]{:S(2)}) copy-start(bf16[64,256]{1,0:T(8,128)(2,1)} %param.25) | copy-start | bytes 98308
  7.2 1348.3 %all-reduce.2.cloned.1.call-start = ((), (), s32[]{:S(2)}) async-start(), calls=%async_computation | async-start | bytes 131072 | tf_op jit(solution)/shard_map/psum | solution.py:156
  9.2 35.4 %collective-permute-start.1 = (bf16[2,64,8,128]{3,2,1,0:T(8,128)(2,1)S(1)}, bf16[2,64,8,128]{3,2,1,0:T(8,128)(2,1)S(1)}, u32[]{:S(2)}, u32[]{:S(2)}) collective-permute-start(bf16[2,64,8,128]{3,2,1,0:T(8,128)(2,1)S(1)} %bitcast_dynamic-update-slice_fusion), channel_id=1, source_target_pairs={{4,0},{8,4},{12,8},{16,12},{20,16},{24,20},{28,24},{32,28},{36,32}... | collective-permute-start | bytes 786440 | tf_op jit(solution)/shard_map/ppermute | solution.py:20
  10.5 34.1 %collective-permute-start = (bf16[2,64,8,128]{3,2,1,0:T(8,128)(2,1)S(1)}, bf16[2,64,8,128]{3,2,1,0:T(8,128)(2,1)S(1)}, u32[]{:S(2)}, u32[]{:S(2)}) collective-permute-start(bf16[2,64,8,128]{3,2,1,0:T(8,128)(2,1)S(1)} %bitcast_dynamic-update-slice_fusion), channel_id=1, source_target_pairs={{0,4},{4,8},{8,12},{12,16},{16,20},{20,24},{24,28},{28,32},{32,36}... | collective-permute-start | bytes 786440 | tf_op jit(solution)/shard_map/ppermute | solution.py:17
  48.4 5.8 copy-start.7
  50.4 7.3 copy-start.11
  60.0 4.0 copy-start.12
  65.8 5.8 copy-start.7
  67.9 7.3 copy-start.11
  77.5 4.0 copy-start.12
  83.3 5.8 copy-start.7
  85.4 7.3 copy-start.11
  95.0 4.0 copy-start.12
  100.8 5.8 copy-start.7
  102.9 7.3 copy-start.11
  112.5 4.0 copy-start.12
  118.3 5.8 copy-start.7
  120.4 7.3 copy-start.11
  130.0 4.0 copy-start.12
  135.8 5.8 copy-start.7
  137.8 7.3 copy-start.11
  147.5 4.0 copy-start.12
  153.3 5.8 copy-start.7
  155.3 7.3 copy-start.11
  170.7 5.8 copy-start.7
  172.8 7.3 copy-start.11
  190.6 5.1 collective-permute-start.3
  191.9 4.2 collective-permute-start.2
  (52 other events, 124.0 us)
Sparse Core Ops, SparseCore 0:
  190.5 1165.0 all-reduce.1
where the time goes:
time: 1370 us; the launch traced here: 1360 us
  waiting for transfers between devices  1160 us (85%)
  local copies, waits for them, and re-layouts  63.2 us (5%)
  other arithmetic  51.8 us (4%)
  matrix products  37.2 us (3%)
  blocking collectives  28.8 us (2%)
  between operations  14.3 us (1%)
    psum x1, waiting for transfers between devices, shards(): grad_w_out = lax.psum(partial_w, 'band')  1160 us
    all_gather x1, blocking collectives, shards(): full_grad = lax.all_gather(grad_out, 'head', axis=0, tiled=True)  28.8 us
  transfers between devices with their start and end apart: 5, of which 2 were waited for; matrix products, arithmetic and copies ran while one was open for 0% of the time, Pallas kernels for 0%

commit v1 on v0

--- a/solution.py
+++ b/solution.py
@@ -153,7 +153,7 @@
     grad_values = owned[1].reshape(chans, blocks * BLOCK).astype(jnp.bfloat16)
     attended = att_all.reshape(chans, blocks * BLOCK)
     partial_w = jnp.einsum("ct,dt->cd", attended, full_grad, preferred_element_type=jnp.float32)
-    grad_w_out = lax.psum(partial_w, "band")
+    grad_w_out = jnp.sum(lax.all_gather(partial_w, "band"), axis=0)
     return (grad_queries, grad_keys, grad_values, grad_w_out)
 
 

time: 1370 us -> 454 us (0.33)
  the two profiles are of different devices: /device:TPU:128 before, /device:TPU:1 now
where the time goes in v1:
time: 454 us; the launch traced here: 449 us
  waiting for transfers between devices  198 us (44%)
  other arithmetic  76.1 us (17%)
  local copies, waits for them, and re-layouts  62.2 us (14%)
  matrix products  53 us (12%)
  blocking collectives  27.7 us (6%)
  starting transfers between devices  17.5 us (4%)
  between operations  14.2 us (3%)
    all_gather x1, waiting for transfers between devices, shards(): grad_w_out = jnp.sum(lax.all_gather(partial_w, 'band'), axis=0)  196 us
    all_gather x1, blocking collectives, shards(): full_grad = lax.all_gather(grad_out, 'head', axis=0, tiled=True)  27.7 us
    scatter-add x8, other arithmetic, run_width(): acc_v = acc_v.at[:, slots].add(dvalue)  19 us
    scatter x8, other arithmetic, run_width(): att_all = att_all.at[:, index].set(attended.astype(jnp.bfloat16))  16.1 us
    dot_general x8, matrix products, block_grads(): jnp.einsum('hqk,hdq->hdk', dscores, query_h, preferred_element_type=jnp.f...  14.6 us
    dot_general x8, matrix products, block_grads(): jnp.einsum('hqk,hdk->hdq', dscores, picked_k, preferred_element_type=jnp....  13.6 us
    gather x16, local copies, waits for them, and re-layouts, block_grads(): picked_k = key_ext[:, slots].reshape(heads_here, HEAD_DIM, span)  13.3 us
    gather x16, local copies, waits for them, and re-layouts, block_grads(): picked_v = value_ext[:, slots].reshape(heads_here, HEAD_DIM, span)  13.3 us
  transfers between devices with their start and end apart: 5, of which 3 were waited for; matrix products, arithmetic and copies ran while one was open for 2% of the time, Pallas kernels for 0%

profile of v1, /device:TPU:1, one launch (start us, length us, event | category | flops | bytes accessed | tf_op | source)
XLA Modules:
  0.0 449.3 jit_solution(14129657560128938277)
XLA Ops:
  9.1 8.7 %collective-permute-start.1 = (bf16[2,64,8,128]{3,2,1,0:T(8,128)(2,1)S(1)}, bf16[2,64,8,128]{3,2,1,0:T(8,128)(2,1)S(1)}, u32[]{:S(2)}, u32[]{:S(2)}) collective-permute-start(bf16[2,64,8,128]{3,2,1,0:T(8,128)(2,1)S(1)} %bitcast_dynamic-update-slice_fusion), channel_id=1, source_target_pairs={{4,0},{8,4},{12,8},{16,12},{20,16},{24,20},{28,24},{32,28},{36,32}... | collective-permute-start | bytes 786440 | tf_op jit(solution)/shard_map/ppermute | solution.py:20
  17.9 1.9 collective-permute-start
  22.5 27.7 %all_gather.9 = bf16[256,1024]{1,0:T(8,128)(2,1)S(1)} all-gather(bf16[64,1024]{1,0:T(8,128)(2,1)} %param.24), channel_id=1, replica_groups=mesh['band'=128,'head'=4] {'head'}, dimensions={0}, use_global_device_ids=true | all-gather | bytes 655360 | tf_op jit(solution)/shard_map/all_gather | solution.py:121
  56.2 170.6 %while.26 = (s32[]{:T(128)}, f32[64,24,128]{2,0,1:T(8,128)S(1)}, f32[64,24,128]{2,0,1:T(8,128)}, bf16[64,8,128]{2,0,1:T(8,128)(2,1)}, bf16[64,8,128]{2,0,1:T(8,1...) while((s32[]{:T(128)}, f32[64,24,128]{2,0,1:T(8,128)S(1)}, ...), condition=%wide.region_7.8_spmd.clone, body=%wide.region_0.7_spmd.clone.sunk | while | flops 107143464 | bytes 16098958 | solution.py:110
  64.9 1.8 fusion.90
  69.0 2.4 scatter_fusion.1
  75.5 2.0 constant_dynamic-update-slice_fusion.3
  86.2 1.8 fusion.90
  90.3 2.4 scatter_fusion.1
  96.8 2.0 constant_dynamic-update-slice_fusion.3
  107.5 1.8 fusion.90
  111.6 2.4 scatter_fusion.1
  118.1 2.0 constant_dynamic-update-slice_fusion.3
  128.9 1.8 fusion.90
  133.0 2.4 scatter_fusion.1
  139.5 2.0 constant_dynamic-update-slice_fusion.3
  154.3 2.4 scatter_fusion.1
  160.8 2.0 constant_dynamic-update-slice_fusion.3
  171.5 1.8 fusion.90
  175.6 2.4 scatter_fusion.1
  182.1 2.0 constant_dynamic-update-slice_fusion.3
  192.8 1.8 fusion.90
  196.9 2.4 scatter_fusion.1
  203.4 2.0 constant_dynamic-update-slice_fusion.3
  214.1 1.8 fusion.90
  218.2 2.4 scatter_fusion.1
  224.7 2.0 constant_dynamic-update-slice_fusion.3
  226.7 2.0 fusion.34
  230.1 4.1 collective-permute-start.3
  234.3 2.7 collective-permute-start.2
  242.0 196.0 %all-gather.3.cloned.1.call-done = f32[8192,256]{1,0:T(8,128)} async-done(((f32[64,256]{1,0:T(8,128)}), f32[8192,256]{1,0:T(8,128)}) %all-gather.3.cloned.1.call-update) | async-done | bytes 8388624 | tf_op jit(solution)/shard_map/all_gather | solution.py:156
  438.0 4.5 reduce_sum.35
  (293 shorter events, 138.6 us)
Async XLA Ops:
  7.2 43.9 %copy-start = (bf16[64,1024]{1,0:T(8,128)(2,1)S(1)}, bf16[64,1024]{1,0:T(8,128)(2,1)}, u32[]{:S(2)}) copy-start(bf16[64,1024]{1,0:T(8,128)(2,1)} %param.21) | copy-start | bytes 393220
  7.2 43.0 %copy-start.5 = (bf16[64,256]{1,0:T(8,128)(2,1)S(1)}, bf16[64,256]{1,0:T(8,128)(2,1)}, u32[]{:S(2)}) copy-start(bf16[64,256]{1,0:T(8,128)(2,1)} %param.25) | copy-start | bytes 98308
  7.2 430.8 %all-gather.3.cloned.1.call-start = ((), (), s32[]{:S(2)}) async-start(), calls=%async_computation | async-start | bytes 8454144 | tf_op jit(solution)/shard_map/all_gather | solution.py:156
  9.1 42.6 %collective-permute-start.1 = (bf16[2,64,8,128]{3,2,1,0:T(8,128)(2,1)S(1)}, bf16[2,64,8,128]{3,2,1,0:T(8,128)(2,1)S(1)}, u32[]{:S(2)}, u32[]{:S(2)}) collective-permute-start(bf16[2,64,8,128]{3,2,1,0:T(8,128)(2,1)S(1)} %bitcast_dynamic-update-slice_fusion), channel_id=1, source_target_pairs={{4,0},{8,4},{12,8},{16,12},{20,16},{24,20},{28,24},{32,28},{36,32}... | collective-permute-start | bytes 786440 | tf_op jit(solution)/shard_map/ppermute | solution.py:20
  17.9 33.9 %collective-permute-start = (bf16[2,64,8,128]{3,2,1,0:T(8,128)(2,1)S(1)}, bf16[2,64,8,128]{3,2,1,0:T(8,128)(2,1)S(1)}, u32[]{:S(2)}, u32[]{:S(2)}) collective-permute-start(bf16[2,64,8,128]{3,2,1,0:T(8,128)(2,1)S(1)} %bitcast_dynamic-update-slice_fusion), channel_id=1, source_target_pairs={{0,4},{4,8},{8,12},{12,16},{16,20},{20,24},{24,28},{28,32},{32,36}... | collective-permute-start | bytes 786440 | tf_op jit(solution)/shard_map/ppermute | solution.py:17
  50.2 1.8 copy-start.1
  56.8 3.5 copy-start.4
  57.6 6.4 %copy-start.3 = (bf16[64,1,128]{2,0,1:T(8,128)(2,1)}, bf16[64,1,128]{2,0,1:T(8,128)(2,1)S(1)}, u32[]{:S(2)}) copy-start(bf16[64,1,128]{2,0,1:T(8,128)(2,1)S(1)} %constant_dynamic-slice_fusion.6) | copy-start | bytes 49156 | tf_op jit(solution)/shard_map/while
  78.2 3.5 copy-start.4
  78.9 6.4 %copy-start.3 = (bf16[64,1,128]{2,0,1:T(8,128)(2,1)}, bf16[64,1,128]{2,0,1:T(8,128)(2,1)S(1)}, u32[]{:S(2)}) copy-start(bf16[64,1,128]{2,0,1:T(8,128)(2,1)S(1)} %constant_dynamic-slice_fusion.6) | copy-start | bytes 49156 | tf_op jit(solution)/shard_map/while
  99.5 3.5 copy-start.4
  100.2 6.4 %copy-start.3 = (bf16[64,1,128]{2,0,1:T(8,128)(2,1)}, bf16[64,1,128]{2,0,1:T(8,128)(2,1)S(1)}, u32[]{:S(2)}) copy-start(bf16[64,1,128]{2,0,1:T(8,128)(2,1)S(1)} %constant_dynamic-slice_fusion.6) | copy-start | bytes 49156 | tf_op jit(solution)/shard_map/while
  120.8 3.5 copy-start.4
  121.6 6.4 %copy-start.3 = (bf16[64,1,128]{2,0,1:T(8,128)(2,1)}, bf16[64,1,128]{2,0,1:T(8,128)(2,1)S(1)}, u32[]{:S(2)}) copy-start(bf16[64,1,128]{2,0,1:T(8,128)(2,1)S(1)} %constant_dynamic-slice_fusion.6) | copy-start | bytes 49156 | tf_op jit(solution)/shard_map/while
  142.2 3.5 copy-start.4
  142.9 6.4 %copy-start.3 = (bf16[64,1,128]{2,0,1:T(8,128)(2,1)}, bf16[64,1,128]{2,0,1:T(8,128)(2,1)S(1)}, u32[]{:S(2)}) copy-start(bf16[64,1,128]{2,0,1:T(8,128)(2,1)S(1)} %constant_dynamic-slice_fusion.6) | copy-start | bytes 49156 | tf_op jit(solution)/shard_map/while
  163.5 3.5 copy-start.4
  164.2 6.4 %copy-start.3 = (bf16[64,1,128]{2,0,1:T(8,128)(2,1)}, bf16[64,1,128]{2,0,1:T(8,128)(2,1)S(1)}, u32[]{:S(2)}) copy-start(bf16[64,1,128]{2,0,1:T(8,128)(2,1)S(1)} %constant_dynamic-slice_fusion.6) | copy-start | bytes 49156 | tf_op jit(solution)/shard_map/while
  184.8 3.5 copy-start.4
  185.5 6.4 %copy-start.3 = (bf16[64,1,128]{2,0,1:T(8,128)(2,1)}, bf16[64,1,128]{2,0,1:T(8,128)(2,1)S(1)}, u32[]{:S(2)}) copy-start(bf16[64,1,128]{2,0,1:T(8,128)(2,1)S(1)} %constant_dynamic-slice_fusion.6) | copy-start | bytes 49156 | tf_op jit(solution)/shard_map/while
  206.1 3.5 copy-start.4
  206.8 6.4 %copy-start.3 = (bf16[64,1,128]{2,0,1:T(8,128)(2,1)}, bf16[64,1,128]{2,0,1:T(8,128)(2,1)S(1)}, u32[]{:S(2)}) copy-start(bf16[64,1,128]{2,0,1:T(8,128)(2,1)S(1)} %constant_dynamic-slice_fusion.6) | copy-start | bytes 49156 | tf_op jit(solution)/shard_map/while
  230.0 7.0 %copy-start.2 = (bf16[64,8,128]{2,0,1:T(8,128)(2,1)S(1)}, bf16[64,8,128]{2,0,1:T(8,128)(2,1)}, u32[]{:S(2)}) copy-start(bf16[64,8,128]{2,0,1:T(8,128)(2,1)} %get-tuple-element.290) | copy-start | bytes 393220
  230.1 8.9 %collective-permute-start.3 = (bf16[2,64,8,128]{3,1,2,0:T(8,128)(2,1)S(1)}, bf16[2,64,8,128]{3,1,2,0:T(8,128)(2,1)S(1)}, u32[]{:S(2)}, u32[]{:S(2)}) collective-permute-start(bf16[2,64,8,128]{3,1,2,0:T(8,128)(2,1)S(1)} %pad_maximum_fusion.2), channel_id=1, source_target_pairs={{4,0},{8,4},{12,8},{16,12},{20,16},{24,20},{28,24},{32,28},{36,32}... | collective-permute-start | bytes 786440 | tf_op jit(solution)/shard_map/ppermute | solution.py:28
  234.3 6.0 %collective-permute-start.2 = (bf16[2,64,8,128]{3,1,2,0:T(8,128)(2,1)S(1)}, bf16[2,64,8,128]{3,1,2,0:T(8,128)(2,1)S(1)}, u32[]{:S(2)}, u32[]{:S(2)}) collective-permute-start(bf16[2,64,8,128]{3,1,2,0:T(8,128)(2,1)S(1)} %pad_maximum_fusion.1), channel_id=1, source_target_pairs={{0,4},{4,8},{8,12},{12,16},{16,20},{20,24},{24,28},{28,32},{32,36}... | collective-permute-start | bytes 786440 | tf_op jit(solution)/shard_map/ppermute | solution.py:28
Sparse Core Ops, SparseCore 0:
  228.9 209.0 all-gather.2
